TPU v7x, 256 devices: a whole 4x4x8 slice. The times are simulated.
256 devices in a mesh: row: 16 (over z, core), col: 8 (over x_hi, y), feat: 2 (over x_lo).
Axes of the slice: x: 4 (x_hi: 2, x_lo: 2; x = x_hi * 2 + x_lo), y: 4, z: 8, core: 2. Of those that a mesh axis runs over, the one named last changes fastest.
Arguments:
- features: bfloat16 [65536, 256], P(('col', 'row'), 'feat'), may hold values from -6 to 6
- tile_rows: int32 [16, 8, 256], P('row', 'col'), may hold values from 0 to 31, as said below
- tile_cols: int32 [16, 8, 256], P('row', 'col'), may hold values from 0 to 63
- tile_count: int32 [16, 8], P('row', 'col'), may hold values from 64 to 256, as said below
- tile_values: bfloat16 [16, 8, 256, 128, 128], P('row', 'col'), may hold values from -0.21875 to 0.21875
- weights: bfloat16 [256, 256], replicated, may hold values from -0.375 to 0.375
- cotangent: bfloat16 [65536, 256], P(('row', 'col'), 'feat'), may hold values from -6 to 6
Outputs:
- activated: bfloat16 [65536, 256], P(('row', 'col'), 'feat')
- feature_grad: bfloat16 [65536, 256], P(('col', 'row'), 'feat')
- weight_grad: float32 [256, 256], P('feat')
Inputs may be any that keep to these rules, and one draw needn't show every extreme that they name: `tile_rows`: block rows of a cell, unevenly loaded. `tile_count`: some cell has all 256 slots live.
All inputs are finite; a program needn't handle non-finite values.
Results may differ from a plain program's by a relative error of at most 0.027.
Values may be sent and summed in bfloat16 or wider, within the bound.
A program may use at most 128 MiB of HBM per device.

v0:
```python
import jax
import jax.numpy as jnp
from jax import lax
from jax.sharding import PartitionSpec as P


def shards(features, tile_rows, tile_cols, tile_count, tile_values, weights, cotangent):
    width = tile_values.shape[-1]
    slots = tile_values.shape[2]
    local_tiles = tile_values[0, 0]
    block_rows = tile_rows[0, 0]
    block_cols = tile_cols[0, 0]
    live_mask = (jnp.arange(slots) < tile_count[0, 0]).astype(jnp.float32)
    n_rowdev = lax.axis_size("row")
    n_coldev = lax.axis_size("col")
    local_blocks = features.shape[0] // width
    feat_half = features.shape[1]
    feat_index = lax.axis_index("feat")
    row_blocks = local_blocks * n_coldev
    col_blocks = local_blocks * n_rowdev
    node_total = features.shape[0] * n_rowdev * n_coldev
    panel = lax.all_gather(features, "row", axis=0, tiled=True)
    gathered = panel.reshape(col_blocks, width, feat_half)[block_cols]
    products = jnp.einsum("tij,tjf->tif", local_tiles, gathered, preferred_element_type=jnp.float32)
    products = products * live_mask[:, None, None]
    partial_value = (
        jnp.zeros((row_blocks, width, feat_half), jnp.float32).at[block_rows].add(products)
    )
    summed = lax.psum_scatter(
        partial_value.reshape(row_blocks * width, feat_half).astype(jnp.bfloat16),
        "col",
        scatter_dimension=0,
        tiled=True,
    )
    weight_rows = lax.dynamic_slice_in_dim(weights, feat_index * feat_half, feat_half, 0)
    mix_term = jnp.dot(summed, weight_rows, preferred_element_type=jnp.float32)
    hidden = lax.psum_scatter(
        mix_term.astype(jnp.bfloat16), "feat", scatter_dimension=1, tiled=True
    ).astype(jnp.float32)
    negative = jnp.minimum(hidden, 0.0)
    activated = jnp.where(hidden > 0, hidden, jnp.expm1(negative)).astype(jnp.bfloat16)
    slope_factor = jnp.where(hidden > 0, 1.0, jnp.exp(negative))
    grad_out = (cotangent.astype(jnp.float32) * slope_factor).astype(jnp.bfloat16)
    grad_whole = lax.all_gather(grad_out, "feat", axis=1, tiled=True)
    weight_term = lax.dot_general(
        summed, grad_whole, (((0,), (0,)), ((), ())), preferred_element_type=jnp.float32
    )
    n_feat = lax.axis_size("feat")
    slots = jnp.zeros((n_feat,) + weight_term.shape, jnp.float32)
    slots = lax.dynamic_update_slice_in_dim(slots, weight_term[None], feat_index, 0)
    slots = lax.psum(slots, ("row", "col", "feat"))
    weight_grad = lax.dynamic_index_in_dim(slots, feat_index, 0, keepdims=False) * node_total ** (
        -0.5
    )
    spread = lax.dot_general(
        grad_whole, weight_rows, (((1,), (1,)), ((), ())), preferred_element_type=jnp.float32
    ).astype(jnp.bfloat16)
    spread_panel = lax.all_gather(spread, "col", axis=0, tiled=True)
    spread_blocks = spread_panel.reshape(row_blocks, width, feat_half)[block_rows]
    back_products = jnp.einsum(
        "tji,tjf->tif", local_tiles, spread_blocks, preferred_element_type=jnp.float32
    )
    back_products = back_products * live_mask[:, None, None]
    back_partial = (
        jnp.zeros((col_blocks, width, feat_half), jnp.float32).at[block_cols].add(back_products)
    )
    back_summed = lax.psum_scatter(
        back_partial.reshape(col_blocks * width, feat_half).astype(jnp.bfloat16),
        "row",
        scatter_dimension=0,
        tiled=True,
    )
    return (activated, back_summed, weight_grad)


def solution(mesh):
    return jax.shard_map(
        shards,
        mesh=mesh,
        in_specs=(
            P(("col", "row"), "feat"),
            P("row", "col", None),
            P("row", "col", None),
            P("row", "col"),
            P("row", "col", None, None, None),
            P(),
            P(("row", "col"), "feat"),
        ),
        out_specs=(P(("row", "col"), "feat"), P(("col", "row"), "feat"), P("feat", None)),
        check_vma=False,
    )
```

profile of v0, /device:TPU:2, one launch (start us, length us, event | category | flops | bytes accessed | tf_op | source)
XLA Modules:
  0.0 605.1 jit_solution(15216501221385841070)
XLA Ops:
  7.2 0.0 copy-start
  7.2 0.0 all-gather.3.cloned.1.call-start
  7.2 0.7 all-gather.3.cloned.1.call-update
  7.9 0.0 reduce-scatter.6.cloned.1.call-start
  8.6 0.7 compare_select_fusion
  9.3 43.2 %all-gather.3.cloned.1.call-done = bf16[8192,128]{1,0:T(8,128)(2,1)} async-done(((bf16[512,128]{1,0:T(8,128)(2,1)}), bf16[8192,128]{1,0:T(8,128)(2,1)}) %all-gather.3.cloned.1.call-update) | async-done | bytes 2097168 | tf_op jit(solution)/shard_map/all_gather | solution.py:22
  52.6 10.2 %gather_fusion = bf16[256,128,128]{2,1,0:T(8,128)(2,1)} fusion(bf16[64,128,128]{2,1,0:T(8,128)(2,1)} %bitcast.36, s32[1024]{0:T(1024)S(1)} %pad_clamp_fusion.1), kind=kCustom, calls=%fused_computation | custom fusion | bytes 16778240 | tf_op jit(solution)/shard_map/gather | solution.py:23
  62.8 13.0 %multiply_bitcast_fusion.1 = f32[256,128,128]{1,2,0:T(8,128)} fusion(bf16[256,128,128]{2,1,0:T(8,128)(2,1)} %gather_fusion, bf16[1,1,256,128,128]{4,3,2,1,0:T(8,128)(2,1)} %param.11, f32[256]{0:T(256)S(1)} %compare_convert_fusion), kind=kOutput, calls=%fused_computation.5 | convolution fusion | flops 1077936128 | bytes 33555456 | tf_op jit(solution)/shard_map/tij,tjf->tif/dot_general | solution.py:24
  75.8 17.4 %copy.17 = f32[256,128,128]{2,1,0:T(8,128)} copy(f32[256,128,128]{1,2,0:T(8,128)} %multiply_bitcast_fusion.1) | data formatting | bytes 33554432 | tf_op jit(solution)/shard_map/mul | solution.py:25
  93.2 0.2 broadcast_in_dim.22
  93.5 0.0 copy-start.3
  93.5 33.2 %scatter_fusion = f32[32,128,128]{2,1,0:T(8,128)S(1)} fusion(f32[32,128,128]{2,1,0:T(8,128)S(1)} %broadcast_in_dim.22, s32[256]{0:T(256)S(1)} %bitcast.43, f32[256,128,128]{2,1,0:T(8,128)} %copy.17), kind=kCustom, calls=%fused_computation.2 | custom fusion | flops 4194304 | bytes 50332672 | tf_op jit(solution)/shard_map/scatter-add | solution.py:27
  126.7 1.1 convert_element_type.38
  127.8 0.0 reduce-scatter.6.cloned.1.call-update
  127.8 0.0 reduce-scatter.10.cloned.1.call-start
  127.9 74.5 %reduce-scatter.6.cloned.1.call-done = bf16[512,128]{1,0:T(8,128)(2,1)} async-done(((bf16[4096,128]{1,0:T(8,128)(2,1)}), bf16[512,128]{1,0:T(8,128)(2,1)}) %reduce-scatter.6.cloned.1.call-update) | async-done | bytes 131088 | tf_op jit(solution)/shard_map/reduce_scatter | solution.py:29
  202.3 0.0 copy-done
  202.4 1.1 convolution_convert_fusion
  203.5 0.8 copy.22
  204.3 0.0 reduce-scatter.10.cloned.1.call-update
  204.3 0.0 all-gather.5.cloned.1.call-start
  204.4 16.0 %reduce-scatter.10.cloned.1.call-done = bf16[128,512]{1,0:T(8,128)(2,1)} async-done(((bf16[256,512]{1,0:T(8,128)(2,1)}), bf16[128,512]{1,0:T(8,128)(2,1)}) %reduce-scatter.10.cloned.1.call-update) | async-done | bytes 131088
  220.4 1.0 copy.23
  221.4 0.0 copy-done.3
  221.5 0.8 fusion.7
  222.3 5.9 all_gather.10
  228.2 0.9 convolution_convert_fusion.1
  229.0 0.0 all-gather.5.cloned.1.call-update
  229.1 0.0 all-reduce.2.cloned.1.call-start
  229.2 1.1 fusion.2
  230.3 0.0 copy-start.2
  230.3 0.7 copy-done.2
  231.0 0.0 all-reduce.2.cloned.1.call-update
  231.0 0.2 reduce-scatter.8.cloned.1.call-start
  231.3 50.6 %all-gather.5.cloned.1.call-done = bf16[4096,128]{1,0:T(8,128)(2,1)} async-done(((bf16[512,128]{1,0:T(8,128)(2,1)}), bf16[4096,128]{1,0:T(8,128)(2,1)}) %all-gather.5.cloned.1.call-update) | async-done | bytes 1048592 | tf_op jit(solution)/shard_map/all_gather | solution.py:58
  281.9 9.8 %gather_fusion.1 = bf16[256,128,128]{2,1,0:T(8,128)(2,1)} fusion(bf16[32,128,128]{2,1,0:T(8,128)(2,1)} %bitcast.35, s32[1024]{0:T(1024)S(1)} %pad_clamp_fusion), kind=kCustom, calls=%fused_computation.1 | custom fusion | bytes 16778240 | tf_op jit(solution)/shard_map/gather | solution.py:59
  291.7 15.4 %multiply_bitcast_fusion = f32[256,128,128]{1,2,0:T(8,128)} fusion(bf16[256,128,128]{2,1,0:T(8,128)(2,1)} %gather_fusion.1, bf16[1,1,256,128,128]{4,3,2,1,0:T(8,128)(2,1)} %param.11, f32[256]{0:T(256)S(1)} %compare_convert_fusion), kind=kOutput, calls=%fused_computation.4 | convolution fusion | flops 1077936128 | bytes 33555456 | tf_op jit(solution)/shard_map/tji,tjf->tif/dot_general | solution.py:60
  307.1 17.5 %copy.19 = f32[256,128,128]{2,1,0:T(8,128)} copy(f32[256,128,128]{1,2,0:T(8,128)} %multiply_bitcast_fusion) | data formatting | bytes 33554432 | tf_op jit(solution)/shard_map/mul | solution.py:63
  324.6 2.5 broadcast_in_dim.23
  327.0 0.0 copy-start.1
  327.0 52.1 %scatter_fusion.1 = f32[64,128,128]{2,1,0:T(8,128)} fusion(f32[64,128,128]{2,1,0:T(8,128)} %broadcast_in_dim.23, s32[256]{0:T(256)S(1)} %bitcast.42, f32[256,128,128]{2,1,0:T(8,128)} %copy.19), kind=kCustom, calls=%fused_computation.3 | custom fusion | flops 4194304 | bytes 50332672 | tf_op jit(solution)/shard_map/scatter-add | solution.py:65
  379.1 3.9 convert_element_type.46
  383.0 0.0 reduce-scatter.8.cloned.1.call-update
  383.1 154.2 %all-reduce.2.cloned.1.call-done = f32[2,128,256]{2,1,0:T(8,128)} async-done(((f32[2,128,256]{2,1,0:T(8,128)}), f32[2,128,256]{2,1,0:T(8,128)}) %all-reduce.2.cloned.1.call-update) | async-done | bytes 262160 | tf_op jit(solution)/shard_map/psum | solution.py:51
  537.3 1.6 multiply_bitcast_fusion.2
  538.8 59.4 %reduce-scatter.8.cloned.1.call-done = bf16[512,128]{1,0:T(8,128)(2,1)} async-done(((bf16[8192,128]{1,0:T(8,128)(2,1)}), bf16[512,128]{1,0:T(8,128)(2,1)}) %reduce-scatter.8.cloned.1.call-update) | async-done | bytes 131088 | tf_op jit(solution)/shard_map/reduce_scatter | solution.py:67
  598.3 0.0 copy-done.1
  (4 shorter events, 0.0 us)
Async XLA Ops:
  7.2 195.2 %copy-start = (bf16[256,256]{1,0:T(8,128)(2,1)S(1)}, bf16[256,256]{1,0:T(8,128)(2,1)}, u32[]{:S(2)}) copy-start(bf16[256,256]{1,0:T(8,128)(2,1)} %param.12) | copy-start | bytes 393220
  7.2 45.4 %all-gather.3.cloned.1.call-start = ((), (), s32[]{:S(2)}) async-start(), calls=%async_computation.3 | async-start | bytes 2228224 | tf_op jit(solution)/shard_map/all_gather | solution.py:22
  7.9 194.4 %reduce-scatter.6.cloned.1.call-start = ((), (), s32[]{:S(2)}) async-start(), calls=%async_computation.4 | async-start | bytes 1179648 | tf_op jit(solution)/shard_map/reduce_scatter | solution.py:29
  93.5 128.0 %copy-start.3 = (bf16[512,128]{1,0:T(8,128)(2,1)S(1)}, bf16[512,128]{1,0:T(8,128)(2,1)}, u32[]{:S(2)}) copy-start(bf16[512,128]{1,0:T(8,128)(2,1)} %param.13) | copy-start | bytes 393220
  127.8 92.6 %reduce-scatter.10.cloned.1.call-start = ((), (), s32[]{:S(2)}) async-start(), calls=%async_computation.8 | async-start | bytes 393216
  204.3 77.5 %all-gather.5.cloned.1.call-start = ((), (), s32[]{:S(2)}) async-start(), calls=%async_computation.5 | async-start | bytes 1179648 | tf_op jit(solution)/shard_map/all_gather | solution.py:58
  229.1 308.2 %all-reduce.2.cloned.1.call-start = ((), (), s32[]{:S(2)}) async-start(), calls=%async_computation.7 | async-start | bytes 524288 | tf_op jit(solution)/shard_map/psum | solution.py:51
  230.3 0.7 copy-start.2
  231.0 367.2 %reduce-scatter.8.cloned.1.call-start = ((), (), s32[]{:S(2)}) async-start(), calls=%async_computation.6 | async-start | bytes 2228224 | tf_op jit(solution)/shard_map/reduce_scatter | solution.py:67
  327.0 271.2 %copy-start.1 = (bf16[256,256]{1,0:T(8,128)(2,1)S(1)}, bf16[256,256]{1,0:T(8,128)(2,1)}, u32[]{:S(2)}) copy-start(bf16[256,256]{1,0:T(8,128)(2,1)} %param.12) | copy-start | bytes 393220
Sparse Core Ops, SparseCore 0:
  9.8 42.6 all-gather.2
  127.9 74.3 reduce-scatter.5
  205.0 15.3 reduce-scatter.9
  229.2 52.6 all-gather.4
  287.2 250.0 all-reduce.1
  540.2 57.9 reduce-scatter.7
where the time goes:
time: 607 us; the launch traced here: 605 us
  waiting for transfers between devices  399 us (66%)
  other arithmetic  93.4 us (15%)
  local copies, waits for them, and re-layouts  60.2 us (10%)
  matrix products  31.5 us (5%)
  between operations  14.9 us (2%)
    psum x1, waiting for transfers between devices, shards(): slots = lax.psum(slots, ('row', 'col', 'feat'))  154 us
    reduce_scatter x1, waiting for transfers between devices, shards(): lax.psum_scatter(partial_value.reshape(row_blocks * width, feat_half).ast...  74.5 us
    reduce_scatter x1, waiting for transfers between devices, shards(): lax.psum_scatter(back_partial.reshape(col_blocks * width, feat_half).asty...  59.4 us
    scatter-add x1, other arithmetic, shards(): jnp.zeros((col_blocks, width, feat_half), jnp.float32).at[block_cols]  52.1 us
    all_gather x1, waiting for transfers between devices, shards(): spread_panel = lax.all_gather(spread, 'col', axis=0, tiled=True)  50.6 us
    all_gather x1, waiting for transfers between devices, shards(): panel = lax.all_gather(features, 'row', axis=0, tiled=True)  43.2 us
    scatter-add x1, other arithmetic, shards(): jnp.zeros((row_blocks, width, feat_half), jnp.float32).at[block_rows]  33.2 us
    mul x1, local copies, waits for them, and re-layouts, shards(): back_products = back_products * live_mask[:, None, None]  17.5 us
  transfers between devices with their start and end apart: 6, of which 6 were waited for; matrix products, arithmetic and copies ran while one was open for 17% of the time, Pallas kernels for 0%

commit v1 on v0

--- a/solution.py
+++ b/solution.py
@@ -55,7 +55,9 @@
     spread = lax.dot_general(
         grad_whole, weight_rows, (((1,), (1,)), ((), ())), preferred_element_type=jnp.float32
     ).astype(jnp.bfloat16)
-    spread_panel = lax.all_gather(spread, "col", axis=0, tiled=True)
+    spread_panel = jnp.concatenate(
+        lax.all_to_all(jnp.stack([spread] * lax.axis_size("col")), "col", 0, 0), axis=0
+    )
     spread_blocks = spread_panel.reshape(row_blocks, width, feat_half)[block_rows]
     back_products = jnp.einsum(
         "tji,tjf->tif", local_tiles, spread_blocks, preferred_element_type=jnp.float32

time: 607 us -> 564 us (0.929)
  waiting for transfers between devices: 399 us -> 351 us
  starting transfers between devices: 0.42 us -> 6.76 us
    all_gather x1 -> x0, waiting for transfers between devices: 50.6 us -> none  [shards(): spread_panel = lax.all_gather(spread, 'col', axis=0, tiled=True)]
    all_to_all x0 -> x1, waiting for transfers between devices: none -> 12.8 us  [shards(): lax.all_to_all(jnp.stack([spread] * lax.axis_size('col')), 'col', 0, 0)]
    psum x1, waiting for transfers between devices: 154 us -> 145 us  [shards(): slots = lax.psum(slots, ('row', 'col', 'feat'))]
    all_to_all x0 -> x1, starting transfers between devices: none -> 6.38 us  [shards(): lax.all_to_all(jnp.stack([spread] * lax.axis_size('col')), 'col', 0, 0)]
    unnamed x7 -> x6, waiting for transfers between devices: 16.8 us -> 16.8 us
  transfers between devices with their start and end apart: 6 -> 6, of which waited for: 6 -> 6; matrix products, arithmetic and copies ran while one was open for 17% -> 18% of each run, Pallas kernels for 0% -> 0%
where the time goes in v1:
time: 564 us; the launch traced here: 563 us
  waiting for transfers between devices  351 us (62%)
  other arithmetic  92.9 us (16%)
  local copies, waits for them, and re-layouts  60.1 us (11%)
  matrix products  30.9 us (5%)
  between operations  14.5 us (3%)
  starting transfers between devices  6.76 us (1%)
  blocking collectives  5.91 us (1%)
    psum x1, waiting for transfers between devices, shards(): slots = lax.psum(slots, ('row', 'col', 'feat'))  145 us
    reduce_scatter x1, waiting for transfers between devices, shards(): lax.psum_scatter(partial_value.reshape(row_blocks * width, feat_half).ast...  74.4 us
    reduce_scatter x1, waiting for transfers between devices, shards(): lax.psum_scatter(back_partial.reshape(col_blocks * width, feat_half).asty...  59.4 us
    scatter-add x1, other arithmetic, shards(): jnp.zeros((col_blocks, width, feat_half), jnp.float32).at[block_cols]  51.6 us
    all_gather x1, waiting for transfers between devices, shards(): panel = lax.all_gather(features, 'row', axis=0, tiled=True)  43.2 us
    scatter-add x1, other arithmetic, shards(): jnp.zeros((row_blocks, width, feat_half), jnp.float32).at[block_rows]  33.2 us
    mul x1, local copies, waits for them, and re-layouts, shards(): back_products = back_products * live_mask[:, None, None]  17.5 us
    mul x1, local copies, waits for them, and re-layouts, shards(): products = products * live_mask[:, None, None]  17.5 us
  transfers between devices with their start and end apart: 6, of which 6 were waited for; matrix products, arithmetic and copies ran while one was open for 18% of the time, Pallas kernels for 0%

profile of v1, /device:TPU:2, one launch (start us, length us, event | category | flops | bytes accessed | tf_op | source)
XLA Modules:
  0.0 562.6 jit_solution(4470569831664324335)
XLA Ops:
  7.2 0.0 copy-start
  7.2 0.0 all-gather.2.cloned.1.call-start
  7.2 0.7 all-gather.2.cloned.1.call-update
  7.9 0.0 reduce-scatter.6.cloned.1.call-start
  8.6 0.7 compare_select_fusion
  9.3 43.2 %all-gather.2.cloned.1.call-done = bf16[8192,128]{1,0:T(8,128)(2,1)} async-done(((bf16[512,128]{1,0:T(8,128)(2,1)}), bf16[8192,128]{1,0:T(8,128)(2,1)}) %all-gather.2.cloned.1.call-update) | async-done | bytes 2097168 | tf_op jit(solution)/shard_map/all_gather | solution.py:22
  52.6 10.2 %gather_fusion = bf16[256,128,128]{2,1,0:T(8,128)(2,1)} fusion(bf16[64,128,128]{2,1,0:T(8,128)(2,1)} %bitcast.36, s32[1024]{0:T(1024)S(1)} %pad_clamp_fusion.1), kind=kCustom, calls=%fused_computation | custom fusion | bytes 16778240 | tf_op jit(solution)/shard_map/gather | solution.py:23
  62.8 13.0 %multiply_bitcast_fusion.1 = f32[256,128,128]{1,2,0:T(8,128)} fusion(bf16[256,128,128]{2,1,0:T(8,128)(2,1)} %gather_fusion, bf16[1,1,256,128,128]{4,3,2,1,0:T(8,128)(2,1)} %param.11, f32[256]{0:T(256)S(1)} %compare_convert_fusion), kind=kOutput, calls=%fused_computation.5 | convolution fusion | flops 1077936128 | bytes 33555456 | tf_op jit(solution)/shard_map/tij,tjf->tif/dot_general | solution.py:24
  75.8 17.5 %copy.17 = f32[256,128,128]{2,1,0:T(8,128)} copy(f32[256,128,128]{1,2,0:T(8,128)} %multiply_bitcast_fusion.1) | data formatting | bytes 33554432 | tf_op jit(solution)/shard_map/mul | solution.py:25
  93.2 0.2 broadcast_in_dim.22
  93.4 0.0 copy-start.3
  93.5 33.2 %scatter_fusion = f32[32,128,128]{2,1,0:T(8,128)S(1)} fusion(f32[32,128,128]{2,1,0:T(8,128)S(1)} %broadcast_in_dim.22, s32[256]{0:T(256)S(1)} %bitcast.43, f32[256,128,128]{2,1,0:T(8,128)} %copy.17), kind=kCustom, calls=%fused_computation.2 | custom fusion | flops 4194304 | bytes 50332672 | tf_op jit(solution)/shard_map/scatter-add | solution.py:27
  126.7 1.1 convert_element_type.38
  127.8 0.0 reduce-scatter.6.cloned.1.call-update
  127.8 0.0 reduce-scatter.10.cloned.1.call-start
  127.9 74.4 %reduce-scatter.6.cloned.1.call-done = bf16[512,128]{1,0:T(8,128)(2,1)} async-done(((bf16[4096,128]{1,0:T(8,128)(2,1)}), bf16[512,128]{1,0:T(8,128)(2,1)}) %reduce-scatter.6.cloned.1.call-update) | async-done | bytes 131088 | tf_op jit(solution)/shard_map/reduce_scatter | solution.py:29
  202.3 0.0 copy-done
  202.3 1.1 convolution_convert_fusion
  203.4 0.8 copy.22
  204.3 0.0 reduce-scatter.10.cloned.1.call-update
  204.3 16.1 %reduce-scatter.10.cloned.1.call-done = bf16[128,512]{1,0:T(8,128)(2,1)} async-done(((bf16[256,512]{1,0:T(8,128)(2,1)}), bf16[128,512]{1,0:T(8,128)(2,1)}) %reduce-scatter.10.cloned.1.call-update) | async-done | bytes 131088
  220.3 1.0 copy.23
  221.4 0.0 copy-done.3
  221.4 0.8 fusion.7
  222.2 5.9 %all_gather.7 = bf16[512,256]{1,0:T(8,128)(2,1)S(1)} all-gather(bf16[512,128]{1,0:T(8,128)(2,1)S(1)} %get-tuple-element.3), channel_id=1, replica_groups=mesh['row'=16,'col'=8,'feat'=2] {'feat'}, dimensions={1}, use_global_device_ids=true | all-gather | bytes 393216 | tf_op jit(solution)/shard_map/all_gather | solution.py:44
  228.1 0.2 convolution_convert_fusion.1
  228.3 1.1 stack.2
  229.4 6.4 %all-to-all-start = ((bf16[8,512,128]{2,1,0:T(8,128)(2,1)}), bf16[8,512,128]{2,1,0:T(8,128)(2,1)S(1)}, u32[]{:S(2)}, u32[]{:S(2)}) async-start(bf16[8,512,128]{2,1,0:T(8,128)(2,1)} %stack.2), calls=%async_computation.1 | async-start | bytes 2097152 | tf_op jit(solution)/shard_map/all_to_all | solution.py:59
  235.8 0.0 all-reduce.2.cloned.1.call-start
  235.9 1.1 fusion.2
  237.0 0.0 copy-start.2
  237.0 0.7 copy-done.2
  237.7 0.0 all-reduce.2.cloned.1.call-update
  237.8 0.2 reduce-scatter.8.cloned.1.call-start
  238.0 12.8 %all-to-all-done = bf16[8,512,128]{2,1,0:T(8,128)(2,1)S(1)} async-done(((bf16[8,512,128]{2,1,0:T(8,128)(2,1)}), bf16[8,512,128]{2,1,0:T(8,128)(2,1)S(1)}, u32[]{:S(2)}, u32[]{:S(2)}) %all-to-all-start) | async-done | bytes 1048608 | tf_op jit(solution)/shard_map/all_to_all | solution.py:59
  250.8 8.6 %gather_fusion.1 = bf16[256,128,128]{2,1,0:T(8,128)(2,1)} fusion(bf16[32,128,128]{2,1,0:T(8,128)(2,1)S(1)} %bitcast.35, s32[1024]{0:T(1024)S(1)} %pad_clamp_fusion), kind=kCustom, calls=%fused_computation.1 | custom fusion | bytes 16778240 | tf_op jit(solution)/shard_map/gather | solution.py:61
  259.4 15.5 %multiply_bitcast_fusion = f32[256,128,128]{1,2,0:T(8,128)} fusion(bf16[256,128,128]{2,1,0:T(8,128)(2,1)} %gather_fusion.1, bf16[1,1,256,128,128]{4,3,2,1,0:T(8,128)(2,1)} %param.11, f32[256]{0:T(256)S(1)} %compare_convert_fusion), kind=kOutput, calls=%fused_computation.4 | convolution fusion | flops 1077936128 | bytes 33555456 | tf_op jit(solution)/shard_map/tji,tjf->tif/dot_general | solution.py:62
  274.9 17.5 %copy.19 = f32[256,128,128]{2,1,0:T(8,128)} copy(f32[256,128,128]{1,2,0:T(8,128)} %multiply_bitcast_fusion) | data formatting | bytes 33554432 | tf_op jit(solution)/shard_map/mul | solution.py:65
  292.4 2.4 broadcast_in_dim.23
  294.8 0.0 copy-start.1
  294.8 51.6 %scatter_fusion.1 = f32[64,128,128]{2,1,0:T(8,128)} fusion(f32[64,128,128]{2,1,0:T(8,128)} %broadcast_in_dim.23, s32[256]{0:T(256)S(1)} %bitcast.42, f32[256,128,128]{2,1,0:T(8,128)} %copy.19), kind=kCustom, calls=%fused_computation.3 | custom fusion | flops 4194304 | bytes 50332672 | tf_op jit(solution)/shard_map/scatter-add | solution.py:67
  346.4 3.9 convert_element_type.46
  350.3 0.0 reduce-scatter.8.cloned.1.call-update
  350.3 144.7 %all-reduce.2.cloned.1.call-done = f32[2,128,256]{2,1,0:T(8,128)} async-done(((f32[2,128,256]{2,1,0:T(8,128)}), f32[2,128,256]{2,1,0:T(8,128)}) %all-reduce.2.cloned.1.call-update) | async-done | bytes 262160 | tf_op jit(solution)/shard_map/psum | solution.py:51
  495.0 1.6 multiply_bitcast_fusion.2
  496.6 59.4 %reduce-scatter.8.cloned.1.call-done = bf16[512,128]{1,0:T(8,128)(2,1)} async-done(((bf16[8192,128]{1,0:T(8,128)(2,1)}), bf16[512,128]{1,0:T(8,128)(2,1)}) %reduce-scatter.8.cloned.1.call-update) | async-done | bytes 131088 | tf_op jit(solution)/shard_map/reduce_scatter | solution.py:69
  556.0 0.0 copy-done.1
  (4 shorter events, 0.0 us)
Async XLA Ops:
  7.2 195.1 %copy-start = (bf16[256,256]{1,0:T(8,128)(2,1)S(1)}, bf16[256,256]{1,0:T(8,128)(2,1)}, u32[]{:S(2)}) copy-start(bf16[256,256]{1,0:T(8,128)(2,1)} %param.12) | copy-start | bytes 393220
  7.2 45.4 %all-gather.2.cloned.1.call-start = ((), (), s32[]{:S(2)}) async-start(), calls=%async_computation.4 | async-start | bytes 2228224 | tf_op jit(solution)/shard_map/all_gather | solution.py:22
  7.9 194.4 %reduce-scatter.6.cloned.1.call-start = ((), (), s32[]{:S(2)}) async-start(), calls=%async_computation.5 | async-start | bytes 1179648 | tf_op jit(solution)/shard_map/reduce_scatter | solution.py:29
  93.4 127.9 %copy-start.3 = (bf16[512,128]{1,0:T(8,128)(2,1)S(1)}, bf16[512,128]{1,0:T(8,128)(2,1)}, u32[]{:S(2)}) copy-start(bf16[512,128]{1,0:T(8,128)(2,1)} %param.13) | copy-start | bytes 393220
  127.8 92.5 %reduce-scatter.10.cloned.1.call-start = ((), (), s32[]{:S(2)}) async-start(), calls=%async_computation.8 | async-start | bytes 393216
  229.4 21.4 %all-to-all-start = ((bf16[8,512,128]{2,1,0:T(8,128)(2,1)}), bf16[8,512,128]{2,1,0:T(8,128)(2,1)S(1)}, u32[]{:S(2)}, u32[]{:S(2)}) async-start(bf16[8,512,128]{2,1,0:T(8,128)(2,1)} %stack.2), calls=%async_computation.1 | async-start | bytes 2097152 | tf_op jit(solution)/shard_map/all_to_all | solution.py:59
  235.8 259.2 %all-reduce.2.cloned.1.call-start = ((), (), s32[]{:S(2)}) async-start(), calls=%async_computation.7 | async-start | bytes 524288 | tf_op jit(solution)/shard_map/psum | solution.py:51
  237.0 0.7 copy-start.2
  237.8 318.3 %reduce-scatter.8.cloned.1.call-start = ((), (), s32[]{:S(2)}) async-start(), calls=%async_computation.6 | async-start | bytes 2228224 | tf_op jit(solution)/shard_map/reduce_scatter | solution.py:69
  294.8 261.2 %copy-start.1 = (bf16[256,256]{1,0:T(8,128)(2,1)S(1)}, bf16[256,256]{1,0:T(8,128)(2,1)}, u32[]{:S(2)}) copy-start(bf16[256,256]{1,0:T(8,128)(2,1)} %param.12) | copy-start | bytes 393220
Sparse Core Ops, SparseCore 0:
  9.8 42.6 all-gather.1
  127.9 74.3 reduce-scatter.5
  204.9 15.3 reduce-scatter.9
  241.8 253.2 all-reduce.1
  498.0 57.9 reduce-scatter.7
